TPU v7x, 32 devices: a whole 2x2x4 slice. The times are simulated.
32 devices in a mesh: dp: 8 (over z, y), tensor: 4 (over x, core).
Axes of the slice: x: 2, y: 2, z: 4, core: 2. Of those that a mesh axis runs over, the one named last changes fastest.
Arguments:
- inputs: bfloat16 [608, 8, 1024], P('tensor', 'dp'), may hold values from -6 to 6
- attn_gain: bfloat16 [2, 1024], P(None, 'dp'), may hold values from 0.5 to 1.5
- attn_shift: bfloat16 [2, 1024], P(None, 'dp'), may hold values from -1.25 to 1.25
- qkv_weight: bfloat16 [2, 1024, 3, 1024], P(None, 'dp', None, 'tensor'), may hold values from -0.1875 to 0.1875
- query_bias: bfloat16 [2, 1024], P(None, 'dp'), may hold values from -3 to 3
- value_bias: bfloat16 [2, 1024], P(None, 'dp'), may hold values from -1.25 to 1.25
- out_weight: bfloat16 [2, 1024, 1024], P(None, 'tensor', 'dp'), may hold values from -2 to 2
- out_bias: bfloat16 [2, 1024], P(None, 'dp'), may hold values from -1.25 to 1.25
- mlp_gain: bfloat16 [2, 1024], P(None, 'dp'), may hold values from 0.5 to 1.5
- mlp_shift: bfloat16 [2, 1024], P(None, 'dp'), may hold values from -1.25 to 1.25
- up_weight: bfloat16 [2, 1024, 4096], P(None, 'dp', 'tensor'), may hold values from -0.1875 to 0.1875
- up_bias: bfloat16 [2, 4096], P(None, 'dp'), may hold values from -1.25 to 1.25
- down_weight: bfloat16 [2, 4096, 1024], P(None, 'tensor', 'dp'), may hold values from -0.09375 to 0.09375
- down_bias: bfloat16 [2, 1024], P(None, 'dp'), may hold values from -1.25 to 1.25
- cotangent: bfloat16 [608, 8, 1024], P('tensor', 'dp'), may hold values from -6 to 6
- image_mask: int32 [8], P('dp'), may hold values 0 or 1
- row_mask: int32 [608, 8], P(None, 'dp'), may hold values from 0 to 1, as said below
Outputs:
- outputs: bfloat16 [608, 8, 1024], P('tensor', 'dp')
- grad_inputs: float32 [608, 8, 1024], P('tensor', 'dp')
- grad_attn_gain: float32 [2, 1024], P(None, 'dp')
- grad_attn_shift: float32 [2, 1024], P(None, 'dp')
- grad_qkv_weight: float32 [2, 1024, 3, 1024], P(None, 'dp', None, 'tensor')
- grad_query_bias: float32 [2, 1024], P(None, 'dp')
- grad_value_bias: float32 [2, 1024], P(None, 'dp')
- grad_out_weight: float32 [2, 1024, 1024], P(None, 'tensor', 'dp')
- grad_out_bias: float32 [2, 1024], P(None, 'dp')
- grad_mlp_gain: float32 [2, 1024], P(None, 'dp')
- grad_mlp_shift: float32 [2, 1024], P(None, 'dp')
- grad_up_weight: float32 [2, 1024, 4096], P(None, 'dp', 'tensor')
- grad_up_bias: float32 [2, 4096], P(None, 'dp')
- grad_down_weight: float32 [2, 4096, 1024], P(None, 'tensor', 'dp')
- grad_down_bias: float32 [2, 1024], P(None, 'dp')
Inputs may be any that keep to these rules, and one draw needn't show every extreme that they name: `row_mask`: row 0 of every image is live; rows 577 and later are 0.
All inputs are finite; a program needn't handle non-finite values. No bound on the sum of `image_mask` on one device may be relied on, other than what follows from the above.
Results may differ from a plain program's by a relative error of at most 0.015.
Values may be sent and summed in bfloat16 or wider, within the bound.
A program may use at most 128 MiB of HBM per device.

v0:
```python
import jax
import jax.numpy as jnp
from jax import lax
from jax.sharding import PartitionSpec as P

HEAD_DIM = 64


def layer_norm(values, gain, shift):
    center = values - jnp.mean(values, -1, keepdims=True)
    inverse = lax.rsqrt(jnp.mean(center * center, -1, keepdims=True) + 1e-05)
    return center * inverse * gain + shift


def norm_backward(values, gain, grad_out):
    center = values - jnp.mean(values, -1, keepdims=True)
    inverse = lax.rsqrt(jnp.mean(center * center, -1, keepdims=True) + 1e-05)
    normal = center * inverse
    grad_hat = grad_out * gain
    grad_in = inverse * (
        grad_hat
        - jnp.mean(grad_hat, -1, keepdims=True)
        - normal * jnp.mean(grad_hat * normal, -1, keepdims=True)
    )
    return (grad_in, jnp.sum(grad_out * normal, (0, 1)), jnp.sum(grad_out, (0, 1)))


def quick_gelu(values):
    return values * jax.nn.sigmoid(1.702 * values)


def gelu_slope(values):
    sigma = jax.nn.sigmoid(1.702 * values)
    return sigma + 1.702 * values * sigma * (1.0 - sigma)


def image_scores(block, keep):
    scores = jnp.einsum(
        "qhe,khe->hqk", block[:, 0], block[:, 1], preferred_element_type=jnp.float32
    )
    scores = scores * HEAD_DIM ** (-0.5)
    return jnp.where(keep[None, None, :], scores, -1e30)


def attention_forward(qkv, row_mask):
    seq_len, images, width = (qkv.shape[0], qkv.shape[1], qkv.shape[3])
    heads = width // HEAD_DIM

    def one_image(which, carry):
        outs, lses = carry
        block = lax.dynamic_index_in_dim(qkv, which, 1, keepdims=False).reshape(
            seq_len, 3, heads, HEAD_DIM
        )
        keep = lax.dynamic_index_in_dim(row_mask, which, 1, keepdims=False) > 0
        scores = image_scores(block, keep)
        row_max = jnp.max(scores, -1, keepdims=True)
        expo = jnp.exp(scores - row_max)
        row_total = jnp.sum(expo, -1, keepdims=True)
        weights = (expo / row_total).astype(jnp.bfloat16)
        values = jnp.einsum(
            "hqk,khe->qhe", weights, block[:, 2], preferred_element_type=jnp.float32
        )
        values = values.astype(jnp.bfloat16).reshape(seq_len, 1, width)
        outs = values
        lses = lax.dynamic_update_index_in_dim(
            lses, (row_max + jnp.log(row_total))[:, :, 0], which, 0
        )
        return (outs, lses)

    start = (
        jnp.zeros((seq_len, images, width), jnp.bfloat16),
        jnp.zeros((images, heads, seq_len), jnp.float32),
    )
    return lax.fori_loop(0, images, one_image, start)


def attention_backward(qkv, lses, grad_mixed, row_mask):
    seq_len, images, width = (qkv.shape[0], qkv.shape[1], qkv.shape[3])
    heads = width // HEAD_DIM
    scale = HEAD_DIM ** (-0.5)

    def one_image(which, grads):
        block = lax.dynamic_index_in_dim(qkv, which, 1, keepdims=False).reshape(
            seq_len, 3, heads, HEAD_DIM
        )
        keep = lax.dynamic_index_in_dim(row_mask, which, 1, keepdims=False) > 0
        grad_out = lax.dynamic_index_in_dim(grad_mixed, which, 1, keepdims=False).reshape(
            seq_len, heads, HEAD_DIM
        )
        lse_here = lax.dynamic_index_in_dim(lses, which, 0, keepdims=False)
        weights = jnp.exp(image_scores(block, keep) - lse_here[:, :, None])
        grad_value = jnp.einsum(
            "hqk,qhe->khe",
            weights.astype(jnp.bfloat16),
            grad_out,
            preferred_element_type=jnp.float32,
        )
        grad_weights = jnp.einsum(
            "qhe,khe->hqk", grad_out, block[:, 2], preferred_element_type=jnp.float32
        )
        delta = jnp.sum(weights * grad_weights, -1, keepdims=True)
        grad_scores = (weights * (grad_weights - delta)).astype(jnp.bfloat16)
        grad_query = (
            jnp.einsum("hqk,khe->qhe", grad_scores, block[:, 1], preferred_element_type=jnp.float32)
            * scale
        )
        grad_key = (
            jnp.einsum("hqk,qhe->khe", grad_scores, block[:, 0], preferred_element_type=jnp.float32)
            * scale
        )
        stacked = jnp.stack([grad_query, grad_key, grad_value], 1).astype(jnp.bfloat16)
        return stacked.reshape(seq_len, 1, 3, width)

    return lax.fori_loop(0, images, one_image, jnp.zeros(qkv.shape, jnp.bfloat16))


def body(
    inputs,
    attn_gain,
    attn_shift,
    qkv_weight,
    query_bias,
    value_bias,
    out_weight,
    out_bias,
    mlp_gain,
    mlp_shift,
    up_weight,
    up_bias,
    down_weight,
    down_bias,
    cotangent,
    image_mask,
    row_mask,
):
    depth_count = qkv_weight.shape[0]
    tensor_rank = lax.axis_index("tensor")
    local_rows = inputs.shape[0]
    head_width = qkv_weight.shape[3]
    unit_width = up_weight.shape[2]
    vectors = jnp.stack(
        [attn_gain, attn_shift, query_bias, value_bias, out_bias, mlp_gain, mlp_shift, down_bias], 1
    )

    def fetch(depth):
        return (
            lax.all_gather(qkv_weight[depth], "dp", axis=0, tiled=True),
            lax.all_gather(up_weight[depth], "dp", axis=0, tiled=True),
            lax.all_gather(out_weight[depth], "dp", axis=1, tiled=True),
            lax.all_gather(down_weight[depth], "dp", axis=1, tiled=True),
            lax.all_gather(vectors[depth], "dp", axis=1, tiled=True),
            lax.all_gather(up_bias[depth], "dp", axis=0, tiled=True),
        )

    def unpack(weights):
        vec = weights[4].astype(jnp.float32)
        query_cols = lax.dynamic_slice_in_dim(vec[2], tensor_rank * head_width, head_width)
        value_cols = lax.dynamic_slice_in_dim(vec[3], tensor_rank * head_width, head_width)
        bias_three = jnp.stack([query_cols, jnp.zeros_like(query_cols), value_cols])
        up_cols = lax.dynamic_slice_in_dim(
            weights[5].astype(jnp.float32), tensor_rank * unit_width, unit_width
        )
        return (vec, bias_three, up_cols)

    def forward_parts(hidden, weights):
        qkv_w, up_w, out_w = (weights[0], weights[1], weights[2])
        vec, bias_three, up_cols = unpack(weights)
        normed = layer_norm(hidden, vec[0], vec[1]).astype(jnp.bfloat16)
        product = jnp.einsum(
            "sid,dce->sice",
            lax.all_gather(normed, "tensor", axis=0, tiled=True),
            qkv_w,
            preferred_element_type=jnp.float32,
        )
        qkv = (product + bias_three).astype(jnp.bfloat16)
        mixed, lses = attention_forward(qkv, row_mask)
        middle = (
            hidden
            + lax.psum_scatter(
                jnp.einsum("sie,ed->sid", mixed, out_w, preferred_element_type=jnp.float32).astype(
                    jnp.bfloat16
                ),
                "tensor",
                scatter_dimension=0,
                tiled=True,
            ).astype(jnp.float32)
            + vec[4]
        )
        normed_mid = layer_norm(middle, vec[5], vec[6]).astype(jnp.bfloat16)
        before = (
            jnp.einsum(
                "sid,df->sif",
                lax.all_gather(normed_mid, "tensor", axis=0, tiled=True),
                up_w,
                preferred_element_type=jnp.float32,
            )
            + up_cols
        )
        active = quick_gelu(before).astype(jnp.bfloat16)
        return (normed, qkv, mixed, lses, middle, normed_mid, before, active)

    hidden = inputs.astype(jnp.float32)
    kept = []
    layer_inputs = []
    stored = []
    for depth in range(depth_count):
        weights = fetch(depth)
        kept.append(weights)
        layer_inputs.append(hidden)
        parts = forward_parts(hidden, weights)
        stored.append(parts)
        down_cols = weights[4][7].astype(jnp.float32)
        mlp_active = parts[7]
        mlp_down_w = weights[3]
        hidden = (
            parts[4]
            + lax.psum_scatter(
                jnp.einsum(
                    "sif,fd->sid", mlp_active, mlp_down_w, preferred_element_type=jnp.float32
                ).astype(jnp.bfloat16),
                "tensor",
                scatter_dimension=0,
                tiled=True,
            ).astype(jnp.float32)
            + down_cols
        )
    live_rows = lax.dynamic_slice_in_dim(row_mask, tensor_rank * local_rows, local_rows, 0)
    live = (live_rows * image_mask[None, :]).astype(jnp.float32)
    grad = cotangent.astype(jnp.float32) * live[:, :, None]
    per_layer = []
    for depth in reversed(range(depth_count)):
        weights = kept[depth]
        parts = stored[depth]
        layer_qkv_w = weights[0]
        layer_up_w = weights[1]
        layer_out_w = weights[2]
        down_w = weights[3]
        layer_vec, layer_bias_three, layer_up_cols = unpack(weights)
        (
            layer_normed,
            layer_qkv,
            layer_mixed,
            layer_lses,
            layer_middle,
            layer_normed_mid,
            layer_before,
            layer_active,
        ) = parts
        full_width = layer_vec.shape[1]
        grad_down_bias = jnp.sum(grad, (0, 1))
        fold_piece = lax.all_gather(grad.astype(jnp.bfloat16), "tensor", axis=0, tiled=True)
        update = jnp.einsum("sid,fd->sif", fold_piece, down_w, preferred_element_type=jnp.float32)
        grad_down_w = jnp.einsum(
            "sif,sid->df", layer_active, fold_piece, preferred_element_type=jnp.float32
        )
        grad_before = (update * gelu_slope(layer_before)).astype(jnp.bfloat16)
        grad_up_cols = jnp.sum(grad_before.astype(jnp.float32), (0, 1))
        grad_up_w = jnp.einsum(
            "sid,sif->df",
            lax.all_gather(layer_normed_mid, "tensor", axis=0, tiled=True),
            grad_before,
            preferred_element_type=jnp.float32,
        )
        grad_normed_mid = lax.psum_scatter(
            jnp.einsum(
                "sif,df->sid", grad_before, layer_up_w, preferred_element_type=jnp.float32
            ).astype(jnp.bfloat16),
            "tensor",
            scatter_dimension=0,
            tiled=True,
        ).astype(jnp.float32)
        grad_mid, grad_mlp_gain, grad_mlp_shift = norm_backward(
            layer_middle, layer_vec[5], grad_normed_mid
        )
        grad_mid = grad_mid + grad
        grad_out_bias = jnp.sum(grad_mid, (0, 1))
        piece = lax.all_gather(grad_mid.astype(jnp.bfloat16), "tensor", axis=0, tiled=True)
        fold_update = jnp.einsum(
            "sid,ed->sie", piece, layer_out_w, preferred_element_type=jnp.float32
        )
        grad_out_w = jnp.einsum(
            "sie,sid->de", layer_mixed, piece, preferred_element_type=jnp.float32
        )
        grad_qkv = attention_backward(
            layer_qkv, layer_lses, fold_update.astype(jnp.bfloat16), row_mask
        )
        grad_bias_three = jnp.sum(grad_qkv.astype(jnp.float32), (0, 1))
        grad_qkv_w = jnp.einsum(
            "sid,sice->dce",
            lax.all_gather(layer_normed, "tensor", axis=0, tiled=True),
            grad_qkv,
            preferred_element_type=jnp.float32,
        )
        grad_normed = lax.psum_scatter(
            jnp.einsum(
                "sice,dce->sid", grad_qkv, layer_qkv_w, preferred_element_type=jnp.float32
            ).astype(jnp.bfloat16),
            "tensor",
            scatter_dimension=0,
            tiled=True,
        ).astype(jnp.float32)
        grad_in, grad_attn_gain, grad_attn_shift = norm_backward(
            layer_inputs[depth], layer_vec[0], grad_normed
        )
        grad_in = grad_in + grad_mid
        empty = jnp.zeros((full_width,), jnp.float32)
        grad_query = lax.dynamic_update_slice_in_dim(
            empty, grad_bias_three[0], tensor_rank * head_width, 0
        )
        grad_value = lax.dynamic_update_slice_in_dim(
            empty, grad_bias_three[2], tensor_rank * head_width, 0
        )
        grad_up_full = lax.dynamic_update_slice_in_dim(
            jnp.zeros((weights[5].shape[0],), jnp.float32),
            grad_up_cols,
            tensor_rank * unit_width,
            0,
        )
        grad_vec = jnp.stack(
            [
                grad_attn_gain,
                grad_attn_shift,
                grad_query,
                grad_value,
                grad_out_bias,
                grad_mlp_gain,
                grad_mlp_shift,
                grad_down_bias,
            ]
        )
        flat = jnp.concatenate(
            [grad_qkv_w.reshape(grad_qkv_w.shape[0], -1), grad_up_w, grad_out_w, grad_down_w], 1
        ).astype(jnp.bfloat16)
        flat = lax.psum_scatter(flat, "dp", scatter_dimension=0, tiled=True).astype(jnp.float32)
        ends = [3 * head_width, 3 * head_width + unit_width, 4 * head_width + unit_width]
        part_qkv, part_up, part_out, part_down = jnp.split(flat, ends, 1)
        shards = (
            part_qkv.reshape(-1, 3, head_width),
            part_up,
            part_out.T,
            part_down.T,
            grad_vec,
            grad_up_full,
        )
        grad = grad_in
        per_layer.insert(0, shards)
    vec_grads = jnp.stack([shards[4] for shards in per_layer])
    bias_grads = jnp.stack([shards[5] for shards in per_layer])
    whole_vec = jnp.concatenate([vec_grads, bias_grads.reshape(depth_count, -1, full_width)], 1)
    whole_vec = lax.psum(whole_vec, ("dp", "tensor"))
    dp_rank = lax.axis_index("dp")
    shard_width = attn_gain.shape[1]
    vec_sum = lax.dynamic_slice_in_dim(whole_vec[:, :8], dp_rank * shard_width, shard_width, 2)
    up_sum = lax.dynamic_slice_in_dim(
        whole_vec[:, 8:].reshape(depth_count, -1), dp_rank * up_bias.shape[1], up_bias.shape[1], 1
    )
    return (
        hidden.astype(jnp.bfloat16),
        grad,
        vec_sum[:, 0],
        vec_sum[:, 1],
        jnp.stack([shards[0] for shards in per_layer]),
        vec_sum[:, 2],
        vec_sum[:, 3],
        jnp.stack([shards[2] for shards in per_layer]),
        vec_sum[:, 4],
        vec_sum[:, 5],
        vec_sum[:, 6],
        jnp.stack([shards[1] for shards in per_layer]),
        up_sum,
        jnp.stack([shards[3] for shards in per_layer]),
        vec_sum[:, 7],
    )


def solution(mesh):
    in_specs = (
        P("tensor", "dp", None),
        P(None, "dp"),
        P(None, "dp"),
        P(None, "dp", None, "tensor"),
        P(None, "dp"),
        P(None, "dp"),
        P(None, "tensor", "dp"),
        P(None, "dp"),
        P(None, "dp"),
        P(None, "dp"),
        P(None, "dp", "tensor"),
        P(None, "dp"),
        P(None, "tensor", "dp"),
        P(None, "dp"),
        P("tensor", "dp", None),
        P("dp"),
        P(None, "dp"),
    )
    out_specs = (
        P("tensor", "dp", None),
        P("tensor", "dp", None),
        P(None, "dp"),
        P(None, "dp"),
        P(None, "dp", None, "tensor"),
        P(None, "dp"),
        P(None, "dp"),
        P(None, "tensor", "dp"),
        P(None, "dp"),
        P(None, "dp"),
        P(None, "dp"),
        P(None, "dp", "tensor"),
        P(None, "dp"),
        P(None, "tensor", "dp"),
        P(None, "dp"),
    )
    return jax.shard_map(body, mesh=mesh, in_specs=in_specs, out_specs=out_specs, check_vma=False)
```

profile of v0, /device:TPU:0, one launch (start us, length us, event | category | flops | bytes accessed | tf_op | source)
XLA Modules:
  0.0 1194.4 jit_solution(9559652890281156475)
XLA Ops:
  14.9 22.4 %all-gather = bf16[1,8,1024]{2,0,1:T(2,128)(2,1)S(1)} all-gather(bf16[1,8,128]{2,0,1:T(2,128)(2,1)S(1)} %get-tuple-element.196), channel_id=2, replica_groups=mesh['dp'=8,'tensor'=4] {'dp'}, dimensions={2}, use_global_device_ids=true | all-gather | bytes 18432 | tf_op jit(solution)/shard_map/all_gather | solution.py:151
  58.0 28.1 %all-gather.2 = bf16[1,256,1024]{2,1,0:T(8,128)(2,1)S(1)} all-gather(bf16[1,256,128]{2,1,0:T(8,128)(2,1)S(1)} %get-tuple-element.173), channel_id=4, replica_groups=mesh['dp'=8,'tensor'=4] {'dp'}, dimensions={2}, use_global_device_ids=true | all-gather | bytes 589824 | tf_op jit(solution)/shard_map/all_gather | solution.py:149
  114.5 24.1 %reduce-scatter.15.cloned.1.call-done = bf16[152,1,1024]{2,0,1:T(8,128)(2,1)} async-done(((bf16[608,1,1024]{2,0,1:T(8,128)(2,1)}), bf16[152,1,1024]{2,0,1:T(8,128)(2,1)}) %reduce-scatter.15.cloned.1.call-update) | async-done | bytes 311312 | tf_op jit(solution)/shard_map/reduce_scatter | solution.py:179
  143.8 26.2 %all-gather.4 = bf16[1,4096]{1,0:T(2,128)(2,1)S(1)} all-gather(bf16[1,512]{1,0:T(2,128)(2,1)S(1)} %get-tuple-element.199), channel_id=6, replica_groups=mesh['dp'=8,'tensor'=4] {'dp'}, dimensions={1}, use_global_device_ids=true | all-gather | bytes 9216 | tf_op jit(solution)/shard_map/all_gather | solution.py:152
  170.0 20.7 %all-gather.45.cloned.1.call-done = bf16[1,1024,1024]{2,1,0:T(8,128)(2,1)} async-done(((bf16[1,128,1024]{2,1,0:T(8,128)(2,1)}), bf16[1,1024,1024]{2,1,0:T(8,128)(2,1)}) %all-gather.45.cloned.1.call-update) | async-done | bytes 2097168 | tf_op jit(solution)/shard_map/all_gather | solution.py:148
  190.7 18.4 %all-gather.29.cloned.1.call-done = bf16[608,1,1024]{2,0,1:T(8,128)(2,1)} async-done(((bf16[152,1,1024]{2,0,1:T(8,128)(2,1)}), bf16[608,1,1024]{2,0,1:T(8,128)(2,1)}) %all-gather.29.cloned.1.call-update) | async-done | bytes 1245200 | tf_op jit(solution)/shard_map/all_gather | solution.py:193
  214.0 48.9 %all-gather.47.cloned.1.call-done = bf16[1,1024,1024]{2,1,0:T(8,128)(2,1)} async-done(((bf16[1,1024,128]{2,1,0:T(8,128)(2,1)}), bf16[1,1024,1024]{2,1,0:T(8,128)(2,1)}) %all-gather.47.cloned.1.call-update) | async-done | bytes 2097168 | tf_op jit(solution)/shard_map/all_gather | solution.py:150
  268.6 23.6 %reduce-scatter.17.cloned.1.call-done = bf16[152,1,1024]{2,0,1:T(8,128)(2,1)} async-done(((bf16[608,1,1024]{2,0,1:T(8,128)(2,1)}), bf16[152,1,1024]{2,0,1:T(8,128)(2,1)}) %reduce-scatter.17.cloned.1.call-update) | async-done | bytes 311312 | tf_op jit(solution)/shard_map/reduce_scatter | solution.py:217
  294.7 29.5 %all-gather.8 = bf16[1,256,1024]{2,1,0:T(8,128)(2,1)S(1)} all-gather(bf16[1,256,128]{2,1,0:T(8,128)(2,1)S(1)} %get-tuple-element.172), channel_id=10, replica_groups=mesh['dp'=8,'tensor'=4] {'dp'}, dimensions={2}, use_global_device_ids=true | all-gather | bytes 589824 | tf_op jit(solution)/shard_map/all_gather | solution.py:149
  341.1 18.8 %all-gather.31.cloned.1.call-done = bf16[608,1,1024]{2,0,1:T(8,128)(2,1)} async-done(((bf16[152,1,1024]{2,0,1:T(8,128)(2,1)}), bf16[608,1,1024]{2,0,1:T(8,128)(2,1)}) %all-gather.31.cloned.1.call-update) | async-done | bytes 1245200 | tf_op jit(solution)/shard_map/all_gather | solution.py:171
  376.5 25.5 %reduce-scatter.19.cloned.1.call-done = bf16[152,1,1024]{2,0,1:T(8,128)(2,1)} async-done(((bf16[608,1,1024]{2,0,1:T(8,128)(2,1)}), bf16[152,1,1024]{2,0,1:T(8,128)(2,1)}) %reduce-scatter.19.cloned.1.call-update) | async-done | bytes 311312 | tf_op jit(solution)/shard_map/reduce_scatter | solution.py:179
  406.6 26.2 %all-gather.10 = bf16[1,4096]{1,0:T(2,128)(2,1)S(1)} all-gather(bf16[1,512]{1,0:T(2,128)(2,1)S(1)} %get-tuple-element.198), channel_id=12, replica_groups=mesh['dp'=8,'tensor'=4] {'dp'}, dimensions={1}, use_global_device_ids=true | all-gather | bytes 9216 | tf_op jit(solution)/shard_map/all_gather | solution.py:152
  432.8 21.5 %all-gather.51.cloned.1.call-done = bf16[1,1024,1024]{2,1,0:T(8,128)(2,1)} async-done(((bf16[1,128,1024]{2,1,0:T(8,128)(2,1)}), bf16[1,1024,1024]{2,1,0:T(8,128)(2,1)}) %all-gather.51.cloned.1.call-update) | async-done | bytes 2097168 | tf_op jit(solution)/shard_map/all_gather | solution.py:148
  454.3 18.4 %all-gather.33.cloned.1.call-done = bf16[608,1,1024]{2,0,1:T(8,128)(2,1)} async-done(((bf16[152,1,1024]{2,0,1:T(8,128)(2,1)}), bf16[608,1,1024]{2,0,1:T(8,128)(2,1)}) %all-gather.33.cloned.1.call-update) | async-done | bytes 1245200 | tf_op jit(solution)/shard_map/all_gather | solution.py:193
  492.8 53.2 %all-gather.53.cloned.1.call-done = bf16[1,1024,1024]{2,1,0:T(8,128)(2,1)} async-done(((bf16[1,1024,128]{2,1,0:T(8,128)(2,1)}), bf16[1,1024,1024]{2,1,0:T(8,128)(2,1)}) %all-gather.53.cloned.1.call-update) | async-done | bytes 2097168 | tf_op jit(solution)/shard_map/all_gather | solution.py:150
  561.4 18.4 %reduce-scatter.23.cloned.1.call-done = bf16[152,1,1024]{2,0,1:T(8,128)(2,1)} async-done(((bf16[608,1,1024]{2,0,1:T(8,128)(2,1)}), bf16[152,1,1024]{2,0,1:T(8,128)(2,1)}) %reduce-scatter.23.cloned.1.call-update) | async-done | bytes 311312 | tf_op jit(solution)/shard_map/reduce_scatter | solution.py:264
  582.8 25.5 %reduce-scatter.21.cloned.1.call-done = bf16[152,1,1024]{2,0,1:T(8,128)(2,1)} async-done(((bf16[608,1,1024]{2,0,1:T(8,128)(2,1)}), bf16[152,1,1024]{2,0,1:T(8,128)(2,1)}) %reduce-scatter.21.cloned.1.call-update) | async-done | bytes 311312 | tf_op jit(solution)/shard_map/reduce_scatter | solution.py:217
  612.1 17.9 %all-gather.37.cloned.1.call-done = bf16[608,1,1024]{2,0,1:T(8,128)(2,1)} async-done(((bf16[152,1,1024]{2,0,1:T(8,128)(2,1)}), bf16[608,1,1024]{2,0,1:T(8,128)(2,1)}) %all-gather.37.cloned.1.call-update) | async-done | bytes 1245200 | tf_op jit(solution)/shard_map/all_gather | solution.py:277
  656.8 26.2 %reduce-scatter.25.cloned.1.call-done = bf16[152,1,1024]{2,0,1:T(8,128)(2,1)} async-done(((bf16[608,1,1024]{2,0,1:T(8,128)(2,1)}), bf16[152,1,1024]{2,0,1:T(8,128)(2,1)}) %reduce-scatter.25.cloned.1.call-update) | async-done | bytes 311312 | tf_op jit(solution)/shard_map/reduce_scatter | solution.py:294
  687.0 17.9 %all-gather.39.cloned.1.call-done = bf16[608,1,1024]{2,0,1:T(8,128)(2,1)} async-done(((bf16[152,1,1024]{2,0,1:T(8,128)(2,1)}), bf16[608,1,1024]{2,0,1:T(8,128)(2,1)}) %all-gather.39.cloned.1.call-update) | async-done | bytes 1245200 | tf_op jit(solution)/shard_map/all_gather | solution.py:251
  714.5 26.0 %reduce-scatter.27.cloned.1.call-done = bf16[152,1,1024]{2,0,1:T(8,128)(2,1)} async-done(((bf16[608,1,1024]{2,0,1:T(8,128)(2,1)}), bf16[152,1,1024]{2,0,1:T(8,128)(2,1)}) %reduce-scatter.27.cloned.1.call-update) | async-done | bytes 311312 | tf_op jit(solution)/shard_map/reduce_scatter | solution.py:264
  853.5 80.5 %all-reduce.2.cloned.1.call-done = f32[2,12,1024]{2,0,1:T(2,128)} async-done(((f32[2,12,1024]{2,0,1:T(2,128)}), f32[2,12,1024]{2,0,1:T(2,128)}) %all-reduce.2.cloned.1.call-update) | async-done | bytes 98320 | tf_op jit(solution)/shard_map/psum | solution.py:350
  936.7 119.5 %reduce-scatter.33.cloned.1.call-done = bf16[128,3072]{1,0:T(8,128)(2,1)} async-done(((bf16[1024,3072]{1,0:T(8,128)(2,1)}), bf16[128,3072]{1,0:T(8,128)(2,1)}) %reduce-scatter.33.cloned.1.call-update) | async-done | bytes 786448
  1059.7 117.3 %reduce-scatter.31.cloned.1.call-done = bf16[128,3072]{1,0:T(8,128)(2,1)} async-done(((bf16[1024,3072]{1,0:T(8,128)(2,1)}), bf16[128,3072]{1,0:T(8,128)(2,1)}) %reduce-scatter.31.cloned.1.call-update) | async-done | bytes 786448
  (383 shorter events, 323.5 us)
Async XLA Ops:
  7.2 78.9 %all-gather.27.cloned.1.call-start = ((), (), s32[]{:S(2)}) async-start(), calls=%async_computation.10 | async-start | bytes 1556480 | tf_op jit(solution)/shard_map/all_gather | solution.py:171
  39.3 63.6 %all-gather.43.cloned.1.call-start = ((), (), s32[]{:S(2)}) async-start(), calls=%async_computation.27 | async-start | bytes 1769472 | tf_op jit(solution)/shard_map/all_gather | solution.py:147
  41.2 97.4 %reduce-scatter.15.cloned.1.call-start = ((), (), s32[]{:S(2)}) async-start(), calls=%async_computation.11 | async-start | bytes 1556480 | tf_op jit(solution)/shard_map/reduce_scatter | solution.py:179
  113.5 77.2 %all-gather.45.cloned.1.call-start = ((), (), s32[]{:S(2)}) async-start(), calls=%async_computation.28 | async-start | bytes 2359296 | tf_op jit(solution)/shard_map/all_gather | solution.py:148
  114.4 94.7 %all-gather.29.cloned.1.call-start = ((), (), s32[]{:S(2)}) async-start(), calls=%async_computation.12 | async-start | bytes 1556480 | tf_op jit(solution)/shard_map/all_gather | solution.py:193
  142.9 120.0 %all-gather.47.cloned.1.call-start = ((), (), s32[]{:S(2)}) async-start(), calls=%async_computation.29 | async-start | bytes 2359296 | tf_op jit(solution)/shard_map/all_gather | solution.py:150
  143.8 148.5 %reduce-scatter.17.cloned.1.call-start = ((), (), s32[]{:S(2)}) async-start(), calls=%async_computation.13 | async-start | bytes 1556480 | tf_op jit(solution)/shard_map/reduce_scatter | solution.py:217
  267.8 73.3 %all-gather.49.cloned.1.call-start = ((), (), s32[]{:S(2)}) async-start(), calls=%async_computation.30 | async-start | bytes 1769472 | tf_op jit(solution)/shard_map/all_gather | solution.py:147
  268.6 91.4 %all-gather.31.cloned.1.call-start = ((), (), s32[]{:S(2)}) async-start(), calls=%async_computation.14 | async-start | bytes 1556480 | tf_op jit(solution)/shard_map/all_gather | solution.py:171
  294.7 107.4 %reduce-scatter.19.cloned.1.call-start = ((), (), s32[]{:S(2)}) async-start(), calls=%async_computation.15 | async-start | bytes 1556480 | tf_op jit(solution)/shard_map/reduce_scatter | solution.py:179
  375.8 78.6 %all-gather.51.cloned.1.call-start = ((), (), s32[]{:S(2)}) async-start(), calls=%async_computation.31 | async-start | bytes 2359296 | tf_op jit(solution)/shard_map/all_gather | solution.py:148
  376.5 96.3 %all-gather.33.cloned.1.call-start = ((), (), s32[]{:S(2)}) async-start(), calls=%async_computation.16 | async-start | bytes 1556480 | tf_op jit(solution)/shard_map/all_gather | solution.py:193
  404.3 88.5 %all-gather.35.cloned.1.call-start = ((), (), s32[]{:S(2)}) async-start(), calls=%async_computation.18 | async-start | bytes 1556480 | tf_op jit(solution)/shard_map/all_gather | solution.py:251
  406.0 140.0 %all-gather.53.cloned.1.call-start = ((), (), s32[]{:S(2)}) async-start(), calls=%async_computation.32 | async-start | bytes 2359296 | tf_op jit(solution)/shard_map/all_gather | solution.py:150
  406.6 173.2 %reduce-scatter.23.cloned.1.call-start = ((), (), s32[]{:S(2)}) async-start(), calls=%async_computation.19 | async-start | bytes 1556480 | tf_op jit(solution)/shard_map/reduce_scatter | solution.py:264
  555.3 53.0 %reduce-scatter.21.cloned.1.call-start = ((), (), s32[]{:S(2)}) async-start(), calls=%async_computation.17 | async-start | bytes 1556480 | tf_op jit(solution)/shard_map/reduce_scatter | solution.py:217
  560.3 69.7 %all-gather.37.cloned.1.call-start = ((), (), s32[]{:S(2)}) async-start(), calls=%async_computation.20 | async-start | bytes 1556480 | tf_op jit(solution)/shard_map/all_gather | solution.py:277
  612.0 71.0 %reduce-scatter.25.cloned.1.call-start = ((), (), s32[]{:S(2)}) async-start(), calls=%async_computation.21 | async-start | bytes 1556480 | tf_op jit(solution)/shard_map/reduce_scatter | solution.py:294
  687.0 53.5 %reduce-scatter.27.cloned.1.call-start = ((), (), s32[]{:S(2)}) async-start(), calls=%async_computation.23 | async-start | bytes 1556480 | tf_op jit(solution)/shard_map/reduce_scatter | solution.py:264
  714.2 48.9 %all-gather.41.cloned.1.call-start = ((), (), s32[]{:S(2)}) async-start(), calls=%async_computation.24 | async-start | bytes 1556480 | tf_op jit(solution)/shard_map/all_gather | solution.py:277
  745.2 62.0 %reduce-scatter.29.cloned.1.call-start = ((), (), s32[]{:S(2)}) async-start(), calls=%async_computation.25 | async-start | bytes 1556480 | tf_op jit(solution)/shard_map/reduce_scatter | solution.py:294
  780.9 153.0 %all-reduce.2.cloned.1.call-start = ((), (), s32[]{:S(2)}) async-start(), calls=%async_computation.26 | async-start | bytes 196608 | tf_op jit(solution)/shard_map/psum | solution.py:350
  809.5 246.7 %reduce-scatter.33.cloned.1.call-start = ((), (), s32[]{:S(2)}) async-start(), calls=%async_computation.34 | async-start | bytes 7077888
  824.0 352.9 %reduce-scatter.31.cloned.1.call-start = ((), (), s32[]{:S(2)}) async-start(), calls=%async_computation.33 | async-start | bytes 7077888
  (79 other events, 1483.6 us)
Sparse Core Ops, SparseCore 0:
  57.3 45.6 all-gather.42
  113.6 24.8 reduce-scatter.14
  141.3 49.3 all-gather.44
  192.8 16.2 all-gather.28
  211.8 51.0 all-gather.46
  267.9 24.2 reduce-scatter.16
  295.0 46.0 all-gather.48
  343.3 16.6 all-gather.30
  375.9 26.1 reduce-scatter.18
  405.0 49.3 all-gather.50
  456.4 16.2 all-gather.32
  475.0 17.8 all-gather.34
  494.9 51.0 all-gather.52
  555.4 24.2 reduce-scatter.22
  582.2 26.1 reduce-scatter.20
  612.1 17.8 all-gather.36
  656.8 26.1 reduce-scatter.24
  687.1 17.7 all-gather.38
  714.4 26.0 reduce-scatter.26
  745.3 17.8 all-gather.40
  781.0 26.1 reduce-scatter.28
  813.4 120.5 all-reduce.1
  937.4 118.7 reduce-scatter.32
  1059.8 117.0 reduce-scatter.30
  (1 shorter events, 15.0 us)
where the time goes:
time: 1200 us; the launch traced here: 1190 us
  waiting for transfers between devices  800 us (67%)
  blocking collectives  149 us (12%)
  matrix products  117 us (10%)
  local copies, waits for them, and re-layouts  59.1 us (5%)
  other arithmetic  51.9 us (4%)
  between operations  16.2 us (1%)
    unnamed x27, waiting for transfers between devices  239 us
    all_gather x2, waiting for transfers between devices, fetch(): lax.all_gather(down_weight[depth], 'dp', axis=1, tiled=True)  102 us
    psum x1, waiting for transfers between devices, body(): whole_vec = lax.psum(whole_vec, ('dp', 'tensor'))  80.5 us
    all_gather x2, blocking collectives, fetch(): lax.all_gather(out_weight[depth], 'dp', axis=1, tiled=True)  57.6 us
    all_gather x2, blocking collectives, fetch(): lax.all_gather(up_bias[depth], 'dp', axis=0, tiled=True)  52.4 us
    reduce_scatter x2, waiting for transfers between devices, forward_parts(): lax.psum_scatter(jnp.einsum('sie,ed->sid', mixed, out_w, preferred_elemen...  49.6 us
    reduce_scatter x2, waiting for transfers between devices, body(): lax.psum_scatter(jnp.einsum('sif,fd->sid', mlp_active, mlp_down_w, prefer...  49.2 us
    reduce_scatter x2, waiting for transfers between devices, body(): lax.psum_scatter(jnp.einsum('sif,df->sid', grad_before, layer_up_w, prefe...  44.4 us
  transfers between devices with their start and end apart: 25, of which 24 were waited for; matrix products, arithmetic and copies ran while one was open for 8% of the time, Pallas kernels for 0%

commit v1 on v0

--- a/solution.py
+++ b/solution.py
@@ -347,7 +347,7 @@
     vec_grads = jnp.stack([shards[4] for shards in per_layer])
     bias_grads = jnp.stack([shards[5] for shards in per_layer])
     whole_vec = jnp.concatenate([vec_grads, bias_grads.reshape(depth_count, -1, full_width)], 1)
-    whole_vec = lax.psum(whole_vec, ("dp", "tensor"))
+    whole_vec = jnp.sum(lax.all_gather(whole_vec, ("dp", "tensor")), axis=0)
     dp_rank = lax.axis_index("dp")
     shard_width = attn_gain.shape[1]
     vec_sum = lax.dynamic_slice_in_dim(whole_vec[:, :8], dp_rank * shard_width, shard_width, 2)

time: 1200 us -> 1140 us (0.950)
  waiting for transfers between devices: 800 us -> 740 us
    psum x1 -> x0, waiting for transfers between devices: 80.5 us -> none  [body(): whole_vec = lax.psum(whole_vec, ('dp', 'tensor'))]
    all_gather x0 -> x1, waiting for transfers between devices: none -> 61.1 us  [body(): whole_vec = jnp.sum(lax.all_gather(whole_vec, ('dp', 'tensor')), axis=0)]
    unnamed x27, waiting for transfers between devices: 239 us -> 206 us
    reduce_scatter x2, waiting for transfers between devices: 40 us -> 26.2 us  [body(): lax.psum_scatter(jnp.einsum('sice,dce->sid', grad_qkv, layer_qkv_w, prefe...]
    unnamed x169 -> x167, local copies, waits for them, and re-layouts: 36.5 us -> 36.5 us
  transfers between devices with their start and end apart: 25 -> 25, of which waited for: 24 -> 23; matrix products, arithmetic and copies ran while one was open for 8% -> 9% of each run, Pallas kernels for 0% -> 0%
where the time goes in v1:
time: 1140 us; the launch traced here: 1130 us
  waiting for transfers between devices  740 us (65%)
  blocking collectives  149 us (13%)
  matrix products  115 us (10%)
  local copies, waits for them, and re-layouts  57.6 us (5%)
  other arithmetic  50.9 us (4%)
  between operations  16.2 us (1%)
    unnamed x27, waiting for transfers between devices  206 us
    all_gather x2, waiting for transfers between devices, fetch(): lax.all_gather(down_weight[depth], 'dp', axis=1, tiled=True)  102 us
    all_gather x1, waiting for transfers between devices, body(): whole_vec = jnp.sum(lax.all_gather(whole_vec, ('dp', 'tensor')), axis=0)  61.1 us
    all_gather x2, blocking collectives, fetch(): lax.all_gather(out_weight[depth], 'dp', axis=1, tiled=True)  57.3 us
    all_gather x2, blocking collectives, fetch(): lax.all_gather(up_bias[depth], 'dp', axis=0, tiled=True)  52.4 us
    reduce_scatter x2, waiting for transfers between devices, forward_parts(): lax.psum_scatter(jnp.einsum('sie,ed->sid', mixed, out_w, preferred_elemen...  49.6 us
    reduce_scatter x2, waiting for transfers between devices, body(): lax.psum_scatter(jnp.einsum('sif,fd->sid', mlp_active, mlp_down_w, prefer...  49.2 us
    reduce_scatter x2, waiting for transfers between devices, body(): lax.psum_scatter(jnp.einsum('sif,df->sid', grad_before, layer_up_w, prefe...  44.4 us
  transfers between devices with their start and end apart: 25, of which 23 were waited for; matrix products, arithmetic and copies ran while one was open for 9% of the time, Pallas kernels for 0%

profile of v1, /device:TPU:0, one launch (start us, length us, event | category | flops | bytes accessed | tf_op | source)
XLA Modules:
  0.0 1130.1 jit_solution(8507920592696934407)
XLA Ops:
  14.9 22.4 %all-gather = bf16[1,8,1024]{2,0,1:T(2,128)(2,1)S(1)} all-gather(bf16[1,8,128]{2,0,1:T(2,128)(2,1)S(1)} %get-tuple-element.211), channel_id=2, replica_groups=mesh['dp'=8,'tensor'=4] {'dp'}, dimensions={2}, use_global_device_ids=true | all-gather | bytes 18432 | tf_op jit(solution)/shard_map/all_gather | solution.py:151
  58.0 28.1 %all-gather.2 = bf16[1,256,1024]{2,1,0:T(8,128)(2,1)S(1)} all-gather(bf16[1,256,128]{2,1,0:T(8,128)(2,1)S(1)} %get-tuple-element.188), channel_id=4, replica_groups=mesh['dp'=8,'tensor'=4] {'dp'}, dimensions={2}, use_global_device_ids=true | all-gather | bytes 589824 | tf_op jit(solution)/shard_map/all_gather | solution.py:149
  114.5 24.1 %reduce-scatter.15.cloned.1.call-done = bf16[152,1,1024]{2,0,1:T(8,128)(2,1)} async-done(((bf16[608,1,1024]{2,0,1:T(8,128)(2,1)}), bf16[152,1,1024]{2,0,1:T(8,128)(2,1)}) %reduce-scatter.15.cloned.1.call-update) | async-done | bytes 311312 | tf_op jit(solution)/shard_map/reduce_scatter | solution.py:179
  143.9 26.2 %all-gather.4 = bf16[1,4096]{1,0:T(2,128)(2,1)S(1)} all-gather(bf16[1,512]{1,0:T(2,128)(2,1)S(1)} %get-tuple-element.214), channel_id=6, replica_groups=mesh['dp'=8,'tensor'=4] {'dp'}, dimensions={1}, use_global_device_ids=true | all-gather | bytes 9216 | tf_op jit(solution)/shard_map/all_gather | solution.py:152
  170.1 20.7 %all-gather.47.cloned.1.call-done = bf16[1,1024,1024]{2,1,0:T(8,128)(2,1)} async-done(((bf16[1,128,1024]{2,1,0:T(8,128)(2,1)}), bf16[1,1024,1024]{2,1,0:T(8,128)(2,1)}) %all-gather.47.cloned.1.call-update) | async-done | bytes 2097168 | tf_op jit(solution)/shard_map/all_gather | solution.py:148
  190.7 18.4 %all-gather.31.cloned.1.call-done = bf16[608,1,1024]{2,0,1:T(8,128)(2,1)} async-done(((bf16[152,1,1024]{2,0,1:T(8,128)(2,1)}), bf16[608,1,1024]{2,0,1:T(8,128)(2,1)}) %all-gather.31.cloned.1.call-update) | async-done | bytes 1245200 | tf_op jit(solution)/shard_map/all_gather | solution.py:193
  214.0 48.9 %all-gather.49.cloned.1.call-done = bf16[1,1024,1024]{2,1,0:T(8,128)(2,1)} async-done(((bf16[1,1024,128]{2,1,0:T(8,128)(2,1)}), bf16[1,1024,1024]{2,1,0:T(8,128)(2,1)}) %all-gather.49.cloned.1.call-update) | async-done | bytes 2097168 | tf_op jit(solution)/shard_map/all_gather | solution.py:150
  268.7 23.6 %reduce-scatter.17.cloned.1.call-done = bf16[152,1,1024]{2,0,1:T(8,128)(2,1)} async-done(((bf16[608,1,1024]{2,0,1:T(8,128)(2,1)}), bf16[152,1,1024]{2,0,1:T(8,128)(2,1)}) %reduce-scatter.17.cloned.1.call-update) | async-done | bytes 311312 | tf_op jit(solution)/shard_map/reduce_scatter | solution.py:217
  294.8 29.1 %all-gather.8 = bf16[1,256,1024]{2,1,0:T(8,128)(2,1)S(1)} all-gather(bf16[1,256,128]{2,1,0:T(8,128)(2,1)S(1)} %get-tuple-element.187), channel_id=10, replica_groups=mesh['dp'=8,'tensor'=4] {'dp'}, dimensions={2}, use_global_device_ids=true | all-gather | bytes 589824 | tf_op jit(solution)/shard_map/all_gather | solution.py:149
  341.4 18.8 %all-gather.33.cloned.1.call-done = bf16[608,1,1024]{2,0,1:T(8,128)(2,1)} async-done(((bf16[152,1,1024]{2,0,1:T(8,128)(2,1)}), bf16[608,1,1024]{2,0,1:T(8,128)(2,1)}) %all-gather.33.cloned.1.call-update) | async-done | bytes 1245200 | tf_op jit(solution)/shard_map/all_gather | solution.py:171
  376.8 25.5 %reduce-scatter.19.cloned.1.call-done = bf16[152,1,1024]{2,0,1:T(8,128)(2,1)} async-done(((bf16[608,1,1024]{2,0,1:T(8,128)(2,1)}), bf16[152,1,1024]{2,0,1:T(8,128)(2,1)}) %reduce-scatter.19.cloned.1.call-update) | async-done | bytes 311312 | tf_op jit(solution)/shard_map/reduce_scatter | solution.py:179
  406.9 26.2 %all-gather.10 = bf16[1,4096]{1,0:T(2,128)(2,1)S(1)} all-gather(bf16[1,512]{1,0:T(2,128)(2,1)S(1)} %get-tuple-element.213), channel_id=12, replica_groups=mesh['dp'=8,'tensor'=4] {'dp'}, dimensions={1}, use_global_device_ids=true | all-gather | bytes 9216 | tf_op jit(solution)/shard_map/all_gather | solution.py:152
  433.1 21.5 %all-gather.53.cloned.1.call-done = bf16[1,1024,1024]{2,1,0:T(8,128)(2,1)} async-done(((bf16[1,128,1024]{2,1,0:T(8,128)(2,1)}), bf16[1,1024,1024]{2,1,0:T(8,128)(2,1)}) %all-gather.53.cloned.1.call-update) | async-done | bytes 2097168 | tf_op jit(solution)/shard_map/all_gather | solution.py:148
  454.6 18.4 %all-gather.35.cloned.1.call-done = bf16[608,1,1024]{2,0,1:T(8,128)(2,1)} async-done(((bf16[152,1,1024]{2,0,1:T(8,128)(2,1)}), bf16[608,1,1024]{2,0,1:T(8,128)(2,1)}) %all-gather.35.cloned.1.call-update) | async-done | bytes 1245200 | tf_op jit(solution)/shard_map/all_gather | solution.py:193
  493.1 53.2 %all-gather.55.cloned.1.call-done = bf16[1,1024,1024]{2,1,0:T(8,128)(2,1)} async-done(((bf16[1,1024,128]{2,1,0:T(8,128)(2,1)}), bf16[1,1024,1024]{2,1,0:T(8,128)(2,1)}) %all-gather.55.cloned.1.call-update) | async-done | bytes 2097168 | tf_op jit(solution)/shard_map/all_gather | solution.py:150
  561.4 18.6 %reduce-scatter.23.cloned.1.call-done = bf16[152,1,1024]{2,0,1:T(8,128)(2,1)} async-done(((bf16[608,1,1024]{2,0,1:T(8,128)(2,1)}), bf16[152,1,1024]{2,0,1:T(8,128)(2,1)}) %reduce-scatter.23.cloned.1.call-update) | async-done | bytes 311312 | tf_op jit(solution)/shard_map/reduce_scatter | solution.py:264
  583.1 25.5 %reduce-scatter.21.cloned.1.call-done = bf16[152,1,1024]{2,0,1:T(8,128)(2,1)} async-done(((bf16[608,1,1024]{2,0,1:T(8,128)(2,1)}), bf16[152,1,1024]{2,0,1:T(8,128)(2,1)}) %reduce-scatter.21.cloned.1.call-update) | async-done | bytes 311312 | tf_op jit(solution)/shard_map/reduce_scatter | solution.py:217
  657.0 26.2 %reduce-scatter.25.cloned.1.call-done = bf16[152,1,1024]{2,0,1:T(8,128)(2,1)} async-done(((bf16[608,1,1024]{2,0,1:T(8,128)(2,1)}), bf16[152,1,1024]{2,0,1:T(8,128)(2,1)}) %reduce-scatter.25.cloned.1.call-update) | async-done | bytes 311312 | tf_op jit(solution)/shard_map/reduce_scatter | solution.py:294
  686.6 17.9 %all-gather.41.cloned.1.call-done = bf16[608,1,1024]{2,0,1:T(8,128)(2,1)} async-done(((bf16[152,1,1024]{2,0,1:T(8,128)(2,1)}), bf16[608,1,1024]{2,0,1:T(8,128)(2,1)}) %all-gather.41.cloned.1.call-update) | async-done | bytes 1245200 | tf_op jit(solution)/shard_map/all_gather | solution.py:251
  714.3 25.8 %reduce-scatter.27.cloned.1.call-done = bf16[152,1,1024]{2,0,1:T(8,128)(2,1)} async-done(((bf16[608,1,1024]{2,0,1:T(8,128)(2,1)}), bf16[152,1,1024]{2,0,1:T(8,128)(2,1)}) %reduce-scatter.27.cloned.1.call-update) | async-done | bytes 311312 | tf_op jit(solution)/shard_map/reduce_scatter | solution.py:264
  744.3 17.9 %all-gather.43.cloned.1.call-done = bf16[608,1,1024]{2,0,1:T(8,128)(2,1)} async-done(((bf16[152,1,1024]{2,0,1:T(8,128)(2,1)}), bf16[608,1,1024]{2,0,1:T(8,128)(2,1)}) %all-gather.43.cloned.1.call-update) | async-done | bytes 1245200 | tf_op jit(solution)/shard_map/all_gather | solution.py:277
  840.3 87.7 %reduce-scatter.33.cloned.1.call-done = bf16[128,3072]{1,0:T(8,128)(2,1)} async-done(((bf16[1024,3072]{1,0:T(8,128)(2,1)}), bf16[128,3072]{1,0:T(8,128)(2,1)}) %reduce-scatter.33.cloned.1.call-update) | async-done | bytes 786448
  931.4 61.1 %all-gather.57.cloned.1.call-done = f32[64,12,1024]{2,1,0:T(8,128)} async-done(((f32[2,12,1024]{2,1,0:T(8,128)}), f32[64,12,1024]{2,1,0:T(8,128)}) %all-gather.57.cloned.1.call-update) | async-done | bytes 3145744 | tf_op jit(solution)/shard_map/all_gather | solution.py:350
  996.4 116.2 %reduce-scatter.31.cloned.1.call-done = bf16[128,3072]{1,0:T(8,128)(2,1)} async-done(((bf16[1024,3072]{1,0:T(8,128)(2,1)}), bf16[128,3072]{1,0:T(8,128)(2,1)}) %reduce-scatter.31.cloned.1.call-update) | async-done | bytes 786448
  (380 shorter events, 311.8 us)
Async XLA Ops:
  7.2 78.9 %all-gather.29.cloned.1.call-start = ((), (), s32[]{:S(2)}) async-start(), calls=%async_computation.10 | async-start | bytes 1556480 | tf_op jit(solution)/shard_map/all_gather | solution.py:171
  39.3 63.6 %all-gather.45.cloned.1.call-start = ((), (), s32[]{:S(2)}) async-start(), calls=%async_computation.26 | async-start | bytes 1769472 | tf_op jit(solution)/shard_map/all_gather | solution.py:147
  41.2 97.4 %reduce-scatter.15.cloned.1.call-start = ((), (), s32[]{:S(2)}) async-start(), calls=%async_computation.11 | async-start | bytes 1556480 | tf_op jit(solution)/shard_map/reduce_scatter | solution.py:179
  113.5 77.2 %all-gather.47.cloned.1.call-start = ((), (), s32[]{:S(2)}) async-start(), calls=%async_computation.27 | async-start | bytes 2359296 | tf_op jit(solution)/shard_map/all_gather | solution.py:148
  114.4 94.7 %all-gather.31.cloned.1.call-start = ((), (), s32[]{:S(2)}) async-start(), calls=%async_computation.12 | async-start | bytes 1556480 | tf_op jit(solution)/shard_map/all_gather | solution.py:193
  142.9 120.0 %all-gather.49.cloned.1.call-start = ((), (), s32[]{:S(2)}) async-start(), calls=%async_computation.28 | async-start | bytes 2359296 | tf_op jit(solution)/shard_map/all_gather | solution.py:150
  143.8 148.5 %reduce-scatter.17.cloned.1.call-start = ((), (), s32[]{:S(2)}) async-start(), calls=%async_computation.13 | async-start | bytes 1556480 | tf_op jit(solution)/shard_map/reduce_scatter | solution.py:217
  267.9 73.5 %all-gather.51.cloned.1.call-start = ((), (), s32[]{:S(2)}) async-start(), calls=%async_computation.29 | async-start | bytes 1769472 | tf_op jit(solution)/shard_map/all_gather | solution.py:147
  268.6 91.6 %all-gather.33.cloned.1.call-start = ((), (), s32[]{:S(2)}) async-start(), calls=%async_computation.14 | async-start | bytes 1556480 | tf_op jit(solution)/shard_map/all_gather | solution.py:171
  294.7 107.6 %reduce-scatter.19.cloned.1.call-start = ((), (), s32[]{:S(2)}) async-start(), calls=%async_computation.15 | async-start | bytes 1556480 | tf_op jit(solution)/shard_map/reduce_scatter | solution.py:179
  376.0 78.6 %all-gather.53.cloned.1.call-start = ((), (), s32[]{:S(2)}) async-start(), calls=%async_computation.30 | async-start | bytes 2359296 | tf_op jit(solution)/shard_map/all_gather | solution.py:148
  376.8 96.3 %all-gather.35.cloned.1.call-start = ((), (), s32[]{:S(2)}) async-start(), calls=%async_computation.16 | async-start | bytes 1556480 | tf_op jit(solution)/shard_map/all_gather | solution.py:193
  404.6 88.5 %all-gather.37.cloned.1.call-start = ((), (), s32[]{:S(2)}) async-start(), calls=%async_computation.18 | async-start | bytes 1556480 | tf_op jit(solution)/shard_map/all_gather | solution.py:251
  406.2 140.0 %all-gather.55.cloned.1.call-start = ((), (), s32[]{:S(2)}) async-start(), calls=%async_computation.31 | async-start | bytes 2359296 | tf_op jit(solution)/shard_map/all_gather | solution.py:150
  406.8 173.2 %reduce-scatter.23.cloned.1.call-start = ((), (), s32[]{:S(2)}) async-start(), calls=%async_computation.19 | async-start | bytes 1556480 | tf_op jit(solution)/shard_map/reduce_scatter | solution.py:264
  555.5 53.0 %reduce-scatter.21.cloned.1.call-start = ((), (), s32[]{:S(2)}) async-start(), calls=%async_computation.17 | async-start | bytes 1556480 | tf_op jit(solution)/shard_map/reduce_scatter | solution.py:217
  560.5 69.7 %all-gather.39.cloned.1.call-start = ((), (), s32[]{:S(2)}) async-start(), calls=%async_computation.20 | async-start | bytes 1556480 | tf_op jit(solution)/shard_map/all_gather | solution.py:277
  612.3 70.9 %reduce-scatter.25.cloned.1.call-start = ((), (), s32[]{:S(2)}) async-start(), calls=%async_computation.21 | async-start | bytes 1556480 | tf_op jit(solution)/shard_map/reduce_scatter | solution.py:294
  686.6 53.6 %reduce-scatter.27.cloned.1.call-start = ((), (), s32[]{:S(2)}) async-start(), calls=%async_computation.23 | async-start | bytes 1556480 | tf_op jit(solution)/shard_map/reduce_scatter | solution.py:264
  713.9 48.4 %all-gather.43.cloned.1.call-start = ((), (), s32[]{:S(2)}) async-start(), calls=%async_computation.24 | async-start | bytes 1556480 | tf_op jit(solution)/shard_map/all_gather | solution.py:277
  744.3 65.1 %reduce-scatter.29.cloned.1.call-start = ((), (), s32[]{:S(2)}) async-start(), calls=%async_computation.25 | async-start | bytes 1556480 | tf_op jit(solution)/shard_map/reduce_scatter | solution.py:294
  780.1 147.9 %reduce-scatter.33.cloned.1.call-start = ((), (), s32[]{:S(2)}) async-start(), calls=%async_computation.34 | async-start | bytes 7077888
  807.5 185.0 %all-gather.57.cloned.1.call-start = ((), (), s32[]{:S(2)}) async-start(), calls=%async_computation.32 | async-start | bytes 4325376 | tf_op jit(solution)/shard_map/all_gather | solution.py:350
  811.6 301.0 %reduce-scatter.31.cloned.1.call-start = ((), (), s32[]{:S(2)}) async-start(), calls=%async_computation.33 | async-start | bytes 7077888
  (77 other events, 1408.6 us)
Sparse Core Ops, SparseCore 0:
  57.3 45.6 all-gather.44
  113.6 24.9 reduce-scatter.14
  141.4 49.3 all-gather.46
  192.8 16.2 all-gather.30
  211.8 51.0 all-gather.48
  268.0 24.2 reduce-scatter.16
  295.1 46.2 all-gather.50
  343.5 16.6 all-gather.32
  376.1 26.1 reduce-scatter.18
  405.2 49.3 all-gather.52
  456.7 16.2 all-gather.34
  475.2 17.8 all-gather.36
  495.2 51.0 all-gather.54
  555.7 24.2 reduce-scatter.22
  582.4 26.1 reduce-scatter.20
  612.4 17.8 all-gather.38
  657.0 26.0 reduce-scatter.24
  686.7 17.8 all-gather.40
  714.0 26.1 reduce-scatter.26
  744.4 17.8 all-gather.42
  780.2 26.1 reduce-scatter.28
  809.9 117.9 reduce-scatter.32
  931.2 61.1 all-gather.56
  996.0 116.4 reduce-scatter.30
  (1 shorter events, 15.0 us)
